TPU v7x, 32 devices: a whole 2x2x4 slice. The times are simulated.
32 devices in a mesh: blk: 8 (over z, x), rep: 4 (over y, core).
Axes of the slice: x: 2, y: 2, z: 4, core: 2. Of those that a mesh axis runs over, the one named last changes fastest.
Arguments:
- features: bfloat16 [32768, 128], P('blk'), may hold values from -6 to 6
- weight: bfloat16 [128, 256], replicated, may hold values from -0.5 to 0.5
- bias: float32 [256], replicated, may hold values from -3 to 3
- tile_values: bfloat16 [8, 8, 160, 128, 128], P('blk', 'rep'), may hold values from 0 to 0.041748047
- tile_place: int32 [8, 8, 160], P('blk', 'rep'), may hold values from 0 to 1023, as said below
- tile_count: int32 [8, 8], P('blk', 'rep'), may hold values from 1 to 160, as said below
Outputs:
- activations: bfloat16 [32768, 256], P('blk')
Inputs may be any that keep to these rules, and one draw needn't show every extreme that they name: `tile_place`: within one pair of destination block and section the 160 positions are distinct. `tile_count`: some pair of destination block and section has all 160 slots occupied.
All inputs are finite; a program needn't handle non-finite values.
Results may differ from a plain program's by a relative error of at most 0.0046.
Values may be sent and summed in bfloat16 or wider, within the bound.
A program may use at most 128 MiB of HBM per device.

v0:
```python
import jax
import jax.numpy as jnp
from jax import lax
from jax.sharding import PartitionSpec as P

TILE = 128


def section_terms(source, tiles, place, count):
    row_count = source.shape[0]
    row_tiles = row_count // TILE
    column = place % row_tiles
    target = place // row_tiles
    blocked = source.reshape(row_tiles, TILE, source.shape[1])
    pieces = jnp.take(blocked, column, axis=0)
    products = jnp.einsum("kij,kjf->kif", tiles, pieces, preferred_element_type=jnp.float32)
    slot_ids = jnp.arange(place.shape[0], dtype=jnp.int32)
    live = (slot_ids < count).astype(jnp.float32)
    products = products * live[:, None, None]
    summed = jax.ops.segment_sum(products, target, num_segments=row_tiles)
    return summed.reshape(row_count, source.shape[1])


def shards(features, weight, bias, tile_values, tile_place, tile_count):
    row_count = features.shape[0]
    sections = tile_values.shape[1]
    cycle_size = lax.axis_size("blk")
    my_replica = lax.axis_index("rep")
    partial_value = jnp.zeros((row_count, features.shape[1]), jnp.float32)
    piece_rows = row_count // cycle_size
    pieces = features.reshape(cycle_size, piece_rows, features.shape[1])
    holding = lax.all_to_all(pieces, "blk", split_axis=0, concat_axis=0, tiled=True)
    for section_index in range(sections):
        offset = my_replica * sections + section_index
        rolled = jnp.roll(holding, offset, axis=0)
        arrived = lax.all_to_all(rolled, "blk", split_axis=0, concat_axis=0, tiled=True)
        source = arrived.reshape(row_count, features.shape[1])
        partial_value = partial_value + section_terms(
            source,
            tile_values[0, section_index],
            tile_place[0, section_index],
            tile_count[0, section_index],
        )
    summed = lax.psum(partial_value, "rep")
    aggregated = summed.astype(jnp.bfloat16)
    output = jnp.dot(aggregated, weight, preferred_element_type=jnp.float32) + bias
    return jnp.maximum(output, 0.0).astype(jnp.bfloat16)


def solution(mesh):
    in_specs = (
        P("blk", None),
        P(),
        P(),
        P("blk", "rep", None, None, None),
        P("blk", "rep", None),
        P("blk", "rep"),
    )
    out_specs = P("blk", None)
    return jax.shard_map(shards, mesh=mesh, in_specs=in_specs, out_specs=out_specs, check_vma=False)
```

profile of v0, /device:TPU:1, one launch (start us, length us, event | category | flops | bytes accessed | tf_op | source)
XLA Modules:
  0.0 222.3 jit_solution(2415213686946378558)
XLA Ops:
  0.0 0.0 copy-start
  0.0 6.5 %all-to-all-start = ((bf16[8,512,128]{2,1,0:T(8,128)(2,1)}), bf16[8,512,128]{2,1,0:T(8,128)(2,1)S(1)}, u32[]{:S(2)}, u32[]{:S(2)}) async-start(bf16[8,512,128]{2,1,0:T(8,128)(2,1)} %bitcast.45), calls=%async_computation | async-start | bytes 2097152 | tf_op jit(solution)/shard_map/all_to_all | solution.py:32
  6.5 25.0 %all-to-all-done = bf16[8,512,128]{2,1,0:T(8,128)(2,1)S(1)} async-done(((bf16[8,512,128]{2,1,0:T(8,128)(2,1)}), bf16[8,512,128]{2,1,0:T(8,128)(2,1)S(1)}, u32[]{:S(2)}, u32[]{:S(2)}) %all-to-all-start) | async-done | bytes 1048608 | tf_op jit(solution)/shard_map/all_to_all | solution.py:32
  31.4 0.1 constant_dynamic-update-slice_fusion.1
  31.5 0.0 copy-start.2
  31.5 0.0 copy-start.3
  31.5 0.1 constant_dynamic-update-slice_fusion
  31.7 1.1 constant_dynamic-slice_fusion
  32.8 29.1 %all_to_all.15 = bf16[8,512,128]{2,1,0:T(8,128)(2,1)S(1)} all-to-all(bf16[8,512,128]{2,1,0:T(8,128)(2,1)S(1)} %get-tuple-element.11), channel_id=1, replica_groups=mesh['blk'=8,'rep'=4] {'blk'}, dimensions={0} | all-to-all | bytes 2097152 | tf_op jit(solution)/shard_map/all_to_all | solution.py:36
  61.9 4.3 %all-to-all-start.1 = ((bf16[8,512,128]{2,1,0:T(8,128)(2,1)}), bf16[8,512,128]{2,1,0:T(8,128)(2,1)S(1)}, u32[]{:S(2)}, u32[]{:S(2)}) async-start(bf16[8,512,128]{2,1,0:T(8,128)(2,1)} %get-tuple-element.12), calls=%async_computation.1 | async-start | bytes 2097152 | tf_op jit(solution)/shard_map/all_to_all | solution.py:36
  66.2 0.0 copy-done.2
  66.2 0.0 copy-done.3
  66.2 0.7 fusion.28
  66.9 0.7 compare_and_fusion
  67.6 0.6 compare_and_fusion.1
  68.2 7.7 %gather_fusion.1 = bf16[160,128,128]{2,1,0:T(8,128)(2,1)} fusion(bf16[32,128,128]{2,1,0:T(8,128)(2,1)S(1)} %bitcast.43, s32[1024]{0:T(1024)S(1)} %pad_clamp_fusion), kind=kCustom, calls=%fused_computation.1.clone | custom fusion | bytes 10486400 | tf_op jit(solution)/shard_map/jit(_take)/gather | solution.py:15
  75.9 11.8 %multiply_bitcast_fusion = f32[160,128,128]{1,2,0:T(8,128)} fusion(f32[160]{0:T(256)S(1)} %get-tuple-element.20, bf16[1,2,160,128,128]{4,3,2,1,0:T(8,128)(2,1)} %param.13, bf16[160,128,128]{2,1,0:T(8,128)(2,1)} %gather_fusion.1, pred[160]{0:T(512)(128)(4,1)S(1)} %get-tuple-element.6), kind=kOutput, calls=%fused_computation.4 | convolution fusion | flops 676331520 | bytes 20972320 | tf_op jit(solution)/shard_map/kij,kjf->kif/dot_general | solution.py:16
  87.7 11.7 %copy.12 = f32[160,128,128]{2,1,0:T(8,128)} copy(f32[160,128,128]{1,2,0:T(8,128)} %multiply_bitcast_fusion) | data formatting | bytes 20971520 | tf_op jit(solution)/shard_map/mul | solution.py:19
  99.5 0.0 all-to-all-done.1
  99.5 7.7 %gather_fusion = bf16[160,128,128]{2,1,0:T(8,128)(2,1)} fusion(bf16[32,128,128]{2,1,0:T(8,128)(2,1)S(1)} %bitcast.42, s32[1024]{0:T(1024)S(1)} %pad_clamp_fusion.1), kind=kCustom, calls=%fused_computation.clone | custom fusion | bytes 10486400 | tf_op jit(solution)/shard_map/jit(_take)/gather | solution.py:15
  107.2 11.8 %multiply_bitcast_fusion.1 = f32[160,128,128]{1,2,0:T(8,128)} fusion(f32[160]{0:T(256)S(1)} %get-tuple-element.19, bf16[1,2,160,128,128]{4,3,2,1,0:T(8,128)(2,1)} %param.13, bf16[160,128,128]{2,1,0:T(8,128)(2,1)} %gather_fusion, pred[160]{0:T(512)(128)(4,1)S(1)} %get-tuple-element.9), kind=kOutput, calls=%fused_computation.5 | convolution fusion | flops 676331520 | bytes 20972320 | tf_op jit(solution)/shard_map/kij,kjf->kif/dot_general | solution.py:16
  119.0 11.7 %copy.10 = f32[160,128,128]{2,1,0:T(8,128)} copy(f32[160,128,128]{1,2,0:T(8,128)} %multiply_bitcast_fusion.1) | data formatting | bytes 20971520 | tf_op jit(solution)/shard_map/mul | solution.py:19
  130.7 0.2 broadcast.127.clone.1
  131.0 21.2 %scatter_fusion.1 = f32[32,128,128]{2,1,0:T(8,128)S(1)} fusion(f32[32,128,128]{2,1,0:T(8,128)S(1)} %broadcast.127.clone.1, s32[160]{0:T(256)S(1)} %bitcast.47, f32[160,128,128]{2,1,0:T(8,128)} %copy.12), kind=kCustom, calls=%fused_computation.3 | custom fusion | flops 2621440 | bytes 31457920 | tf_op jit(solution)/shard_map/scatter-add | solution.py:20
  152.2 0.0 copy-start.1
  152.2 1.3 copy-done.1
  153.5 0.2 broadcast.127.clone
  153.7 21.2 %scatter_fusion = f32[32,128,128]{2,1,0:T(8,128)S(1)} fusion(f32[32,128,128]{2,1,0:T(8,128)S(1)} %broadcast.127.clone, s32[160]{0:T(256)S(1)} %bitcast.46, f32[160,128,128]{2,1,0:T(8,128)} %copy.10), kind=kCustom, calls=%fused_computation.2 | custom fusion | flops 2621440 | bytes 31457920 | tf_op jit(solution)/shard_map/scatter-add | solution.py:20
  174.9 0.0 copy-start.4
  174.9 3.2 %add.66 = f32[32,128,128]{2,1,0:T(8,128)} add(f32[32,128,128]{2,1,0:T(8,128)S(1)} %scatter_fusion, f32[32,128,128]{2,1,0:T(8,128)} %copy-done.1) | non-fusion elementwise | flops 524288 | bytes 6291456 | tf_op jit(solution)/shard_map/add | solution.py:38
  178.1 42.2 %all-reduce.1 = bf16[4096,128]{1,0:T(8,128)(2,1)S(1)} all-reduce(f32[4096,128]{1,0:T(8,128)} %bitcast.44), channel_id=1, replica_groups=mesh['blk'=8,'rep'=4] {'rep'}, use_global_device_ids=true, to_apply=%region_2.5 | all-reduce | flops 524288 | bytes 3145728 | tf_op jit(solution)/shard_map/psum | solution.py:44
  220.3 2.0 fusion.11
  (6 shorter events, 0.0 us)
Async XLA Ops:
  0.0 220.3 %copy-start = (bf16[128,256]{1,0:T(8,128)(2,1)S(1)}, bf16[128,256]{1,0:T(8,128)(2,1)}, u32[]{:S(2)}) copy-start(bf16[128,256]{1,0:T(8,128)(2,1)} %param.11) | copy-start | bytes 196612
  0.0 31.4 %all-to-all-start = ((bf16[8,512,128]{2,1,0:T(8,128)(2,1)}), bf16[8,512,128]{2,1,0:T(8,128)(2,1)S(1)}, u32[]{:S(2)}, u32[]{:S(2)}) async-start(bf16[8,512,128]{2,1,0:T(8,128)(2,1)} %bitcast.45), calls=%async_computation | async-start | bytes 2097152 | tf_op jit(solution)/shard_map/all_to_all | solution.py:32
  31.5 34.7 %copy-start.2 = (s32[1,2,160]{2,1,0:T(2,128)S(1)}, s32[1,2,160]{2,1,0:T(2,128)}, u32[]{:S(2)}) copy-start(s32[1,2,160]{2,1,0:T(2,128)} %param.14) | copy-start | bytes 3844
  31.5 34.7 %copy-start.3 = (s32[1,2]{1,0:T(1,128)S(1)}, s32[1,2]{1,0:T(1,128)}, u32[]{:S(2)}) copy-start(s32[1,2]{1,0:T(1,128)} %param.15) | copy-start | bytes 28
  61.9 37.5 %all-to-all-start.1 = ((bf16[8,512,128]{2,1,0:T(8,128)(2,1)}), bf16[8,512,128]{2,1,0:T(8,128)(2,1)S(1)}, u32[]{:S(2)}, u32[]{:S(2)}) async-start(bf16[8,512,128]{2,1,0:T(8,128)(2,1)} %get-tuple-element.12), calls=%async_computation.1 | async-start | bytes 2097152 | tf_op jit(solution)/shard_map/all_to_all | solution.py:36
  152.2 1.3 copy-start.1
  174.9 45.4 %copy-start.4 = (f32[256]{0:T(256)S(1)}, f32[256]{0:T(256)}, u32[]{:S(2)}) copy-start(f32[256]{0:T(256)} %param.12) | copy-start | bytes 3076
where the time goes:
time: 224 us; the launch traced here: 222 us
  blocking collectives  71.3 us (32%)
  other arithmetic  46.8 us (21%)
  local copies, waits for them, and re-layouts  42.7 us (19%)
  matrix products  25.7 us (11%)
  waiting for transfers between devices  25 us (11%)
  starting transfers between devices  10.7 us (5%)
    scatter-add x2, other arithmetic, section_terms(): summed = jax.ops.segment_sum(products, target, num_segments=row_tiles)  42.4 us
    psum x1, blocking collectives, shards(): summed = lax.psum(partial_value, 'rep')  42.2 us
    all_to_all x1, blocking collectives, shards(): lax.all_to_all(rolled, 'blk', split_axis=0, concat_axis=0, tiled=True)  29.1 us
    all_to_all x1, waiting for transfers between devices, shards(): lax.all_to_all(pieces, 'blk', split_axis=0, concat_axis=0, tiled=True)  25 us
    dot_general x2, matrix products, section_terms(): jnp.einsum('kij,kjf->kif', tiles, pieces, preferred_element_type=jnp.floa...  23.6 us
    mul x2, local copies, waits for them, and re-layouts, section_terms(): products = products * live[:, None, None]  23.5 us
    gather x2, local copies, waits for them, and re-layouts, section_terms(): pieces = jnp.take(blocked, column, axis=0)  15.4 us
    all_to_all x1, starting transfers between devices, shards(): lax.all_to_all(pieces, 'blk', split_axis=0, concat_axis=0, tiled=True)  6.47 us
  transfers between devices with their start and end apart: 2, of which 1 were waited for; matrix products, arithmetic and copies ran while one was open for 15% of the time, Pallas kernels for 0%

commit v1 on v0

--- a/solution.py
+++ b/solution.py
@@ -41,7 +41,8 @@
             tile_place[0, section_index],
             tile_count[0, section_index],
         )
-    summed = lax.psum(partial_value, "rep")
+    parts = lax.all_gather(partial_value, "rep")
+    summed = jnp.sum(parts, axis=0)
     aggregated = summed.astype(jnp.bfloat16)
     output = jnp.dot(aggregated, weight, preferred_element_type=jnp.float32) + bias
     return jnp.maximum(output, 0.0).astype(jnp.bfloat16)

time: 224 us -> 272 us (1.21)
  waiting for transfers between devices: 25 us -> 85.8 us
  blocking collectives: 71.3 us -> 29.1 us
  other arithmetic: 46.8 us -> 62.2 us
  between operations: 0.16 us -> 13.5 us
    all_gather x0 -> x1, waiting for transfers between devices: none -> 60.8 us  [shards(): parts = lax.all_gather(partial_value, 'rep')]
    psum x1 -> x0, blocking collectives: 42.2 us -> none  [shards(): summed = lax.psum(partial_value, 'rep')]
    scatter-add x2, other arithmetic: 42.4 us -> 53.6 us  [section_terms(): summed = jax.ops.segment_sum(products, target, num_segments=row_tiles)]
    reduce_sum x0 -> x1, other arithmetic: none -> 4.13 us  [shards(): summed = jnp.sum(parts, axis=0)]
  transfers between devices with their start and end apart: 2 -> 3, of which waited for: 1 -> 2; matrix products, arithmetic and copies ran while one was open for 15% -> 12% of each run, Pallas kernels for 0% -> 0%
where the time goes in v1:
time: 272 us; the launch traced here: 270 us
  waiting for transfers between devices  85.8 us (32%)
  other arithmetic  62.2 us (23%)
  local copies, waits for them, and re-layouts  42.7 us (16%)
  blocking collectives  29.1 us (11%)
  matrix products  25.7 us (9%)
  between operations  13.5 us (5%)
  starting transfers between devices  10.8 us (4%)
    all_gather x1, waiting for transfers between devices, shards(): parts = lax.all_gather(partial_value, 'rep')  60.8 us
    scatter-add x2, other arithmetic, section_terms(): summed = jax.ops.segment_sum(products, target, num_segments=row_tiles)  53.6 us
    all_to_all x1, blocking collectives, shards(): lax.all_to_all(rolled, 'blk', split_axis=0, concat_axis=0, tiled=True)  29.1 us
    all_to_all x1, waiting for transfers between devices, shards(): lax.all_to_all(pieces, 'blk', split_axis=0, concat_axis=0, tiled=True)  25 us
    dot_general x2, matrix products, section_terms(): jnp.einsum('kij,kjf->kif', tiles, pieces, preferred_element_type=jnp.floa...  23.7 us
    mul x2, local copies, waits for them, and re-layouts, section_terms(): products = products * live[:, None, None]  23.5 us
    gather x2, local copies, waits for them, and re-layouts, section_terms(): pieces = jnp.take(blocked, column, axis=0)  15.4 us
    all_to_all x1, starting transfers between devices, shards(): lax.all_to_all(pieces, 'blk', split_axis=0, concat_axis=0, tiled=True)  6.47 us
  transfers between devices with their start and end apart: 3, of which 2 were waited for; matrix products, arithmetic and copies ran while one was open for 12% of the time, Pallas kernels for 0%

profile of v1, /device:TPU:1, one launch (start us, length us, event | category | flops | bytes accessed | tf_op | source)
XLA Modules:
  0.0 269.8 jit_solution(15064016022891501216)
XLA Ops:
  6.5 0.0 copy-start
  6.5 6.5 %all-to-all-start = ((bf16[8,512,128]{2,1,0:T(8,128)(2,1)}), bf16[8,512,128]{2,1,0:T(8,128)(2,1)S(1)}, u32[]{:S(2)}, u32[]{:S(2)}) async-start(bf16[8,512,128]{2,1,0:T(8,128)(2,1)} %bitcast.45), calls=%async_computation | async-start | bytes 2097152 | tf_op jit(solution)/shard_map/all_to_all | solution.py:32
  13.0 25.0 %all-to-all-done = bf16[8,512,128]{2,1,0:T(8,128)(2,1)S(1)} async-done(((bf16[8,512,128]{2,1,0:T(8,128)(2,1)}), bf16[8,512,128]{2,1,0:T(8,128)(2,1)S(1)}, u32[]{:S(2)}, u32[]{:S(2)}) %all-to-all-start) | async-done | bytes 1048608 | tf_op jit(solution)/shard_map/all_to_all | solution.py:32
  38.0 0.1 constant_dynamic-update-slice_fusion.1
  38.0 0.0 copy-start.1
  38.1 0.0 copy-start.2
  38.1 0.1 constant_dynamic-update-slice_fusion
  38.2 1.1 constant_dynamic-slice_fusion
  39.3 29.1 %all_to_all.15 = bf16[8,512,128]{2,1,0:T(8,128)(2,1)S(1)} all-to-all(bf16[8,512,128]{2,1,0:T(8,128)(2,1)S(1)} %get-tuple-element.11), channel_id=1, replica_groups=mesh['blk'=8,'rep'=4] {'blk'}, dimensions={0} | all-to-all | bytes 2097152 | tf_op jit(solution)/shard_map/all_to_all | solution.py:36
  68.5 4.3 %all-to-all-start.1 = ((bf16[8,512,128]{2,1,0:T(8,128)(2,1)}), bf16[8,512,128]{2,1,0:T(8,128)(2,1)S(1)}, u32[]{:S(2)}, u32[]{:S(2)}) async-start(bf16[8,512,128]{2,1,0:T(8,128)(2,1)} %get-tuple-element.12), calls=%async_computation.1 | async-start | bytes 2097152 | tf_op jit(solution)/shard_map/all_to_all | solution.py:36
  72.7 0.0 all-gather.2.cloned.1.call-start
  72.8 0.0 copy-done.2
  72.8 0.7 fusion.28
  73.5 0.7 compare_and_fusion
  74.2 0.6 compare_and_fusion.1
  74.8 7.7 %gather_fusion.1 = bf16[160,128,128]{2,1,0:T(8,128)(2,1)} fusion(bf16[32,128,128]{2,1,0:T(8,128)(2,1)S(1)} %bitcast.43, s32[1024]{0:T(1024)S(1)} %pad_clamp_fusion), kind=kCustom, calls=%fused_computation.1.clone | custom fusion | bytes 10486400 | tf_op jit(solution)/shard_map/jit(_take)/gather | solution.py:15
  82.5 11.8 %multiply_bitcast_fusion = f32[160,128,128]{1,2,0:T(8,128)} fusion(f32[160]{0:T(256)S(1)} %get-tuple-element.20, bf16[1,2,160,128,128]{4,3,2,1,0:T(8,128)(2,1)} %param.13, bf16[160,128,128]{2,1,0:T(8,128)(2,1)} %gather_fusion.1, pred[160]{0:T(512)(128)(4,1)S(1)} %get-tuple-element.6), kind=kOutput, calls=%fused_computation.4 | convolution fusion | flops 676331520 | bytes 20972320 | tf_op jit(solution)/shard_map/kij,kjf->kif/dot_general | solution.py:16
  94.4 11.7 %copy.16 = f32[160,128,128]{2,1,0:T(8,128)} copy(f32[160,128,128]{1,2,0:T(8,128)} %multiply_bitcast_fusion) | data formatting | bytes 20971520 | tf_op jit(solution)/shard_map/mul | solution.py:19
  106.1 0.0 all-to-all-done.1
  106.1 7.7 %gather_fusion = bf16[160,128,128]{2,1,0:T(8,128)(2,1)} fusion(bf16[32,128,128]{2,1,0:T(8,128)(2,1)S(1)} %bitcast.42, s32[1024]{0:T(1024)S(1)} %pad_clamp_fusion.1), kind=kCustom, calls=%fused_computation.clone | custom fusion | bytes 10486400 | tf_op jit(solution)/shard_map/jit(_take)/gather | solution.py:15
  113.8 11.8 %multiply_bitcast_fusion.1 = f32[160,128,128]{1,2,0:T(8,128)} fusion(f32[160]{0:T(256)S(1)} %get-tuple-element.19, bf16[1,2,160,128,128]{4,3,2,1,0:T(8,128)(2,1)} %param.13, bf16[160,128,128]{2,1,0:T(8,128)(2,1)} %gather_fusion, pred[160]{0:T(512)(128)(4,1)S(1)} %get-tuple-element.9), kind=kOutput, calls=%fused_computation.5 | convolution fusion | flops 676331520 | bytes 20972320 | tf_op jit(solution)/shard_map/kij,kjf->kif/dot_general | solution.py:16
  125.6 11.7 %copy.14 = f32[160,128,128]{2,1,0:T(8,128)} copy(f32[160,128,128]{1,2,0:T(8,128)} %multiply_bitcast_fusion.1) | data formatting | bytes 20971520 | tf_op jit(solution)/shard_map/mul | solution.py:19
  137.4 0.2 broadcast.127.clone.1
  137.6 21.2 %scatter_fusion.1 = f32[32,128,128]{2,1,0:T(8,128)S(1)} fusion(f32[32,128,128]{2,1,0:T(8,128)S(1)} %broadcast.127.clone.1, s32[160]{0:T(256)S(1)} %bitcast.47, f32[160,128,128]{2,1,0:T(8,128)} %copy.16), kind=kCustom, calls=%fused_computation.3 | custom fusion | flops 2621440 | bytes 31457920 | tf_op jit(solution)/shard_map/scatter-add | solution.py:20
  158.8 1.6 broadcast.127.clone
  160.4 32.4 %scatter_fusion = f32[32,128,128]{2,1,0:T(8,128)} fusion(f32[32,128,128]{2,1,0:T(8,128)} %broadcast.127.clone, s32[160]{0:T(256)S(1)} %bitcast.46, f32[160,128,128]{2,1,0:T(8,128)} %copy.14), kind=kCustom, calls=%fused_computation.2 | custom fusion | flops 2621440 | bytes 31457920 | tf_op jit(solution)/shard_map/scatter-add | solution.py:20
  192.8 3.2 %add.71 = f32[32,128,128]{2,1,0:T(8,128)} add(f32[32,128,128]{2,1,0:T(8,128)} %scatter_fusion, f32[32,128,128]{2,1,0:T(8,128)S(1)} %scatter_fusion.1) | non-fusion elementwise | flops 524288 | bytes 6291456 | tf_op jit(solution)/shard_map/add | solution.py:38
  195.9 0.0 all-gather.2.cloned.1.call-update
  195.9 0.0 copy-start.3
  195.9 60.8 %all-gather.2.cloned.1.call-done = f32[4,4096,128]{2,1,0:T(8,128)} async-done(((f32[1,4096,128]{2,1,0:T(8,128)}), f32[4,4096,128]{2,1,0:T(8,128)}) %all-gather.2.cloned.1.call-update) | async-done | bytes 8388624 | tf_op jit(solution)/shard_map/all_gather | solution.py:44
  256.8 4.1 %reduce_sum.9 = bf16[4096,128]{1,0:T(8,128)(2,1)S(1)} reduce(f32[4,4096,128]{2,1,0:T(8,128)} %all-gather.2.cloned.1.call-done, f32[]{:T(128)} %constant.69.clone.1), dimensions={0}, to_apply=%region_2.5 | reduce | flops 1572864 | bytes 9437188 | tf_op jit(solution)/shard_map/reduce_sum | solution.py:45
  260.9 2.0 fusion.11
  (7 shorter events, 0.0 us)
Async XLA Ops:
  6.5 254.4 %copy-start = (bf16[128,256]{1,0:T(8,128)(2,1)S(1)}, bf16[128,256]{1,0:T(8,128)(2,1)}, u32[]{:S(2)}) copy-start(bf16[128,256]{1,0:T(8,128)(2,1)} %param.11) | copy-start | bytes 196612
  6.5 31.4 %all-to-all-start = ((bf16[8,512,128]{2,1,0:T(8,128)(2,1)}), bf16[8,512,128]{2,1,0:T(8,128)(2,1)S(1)}, u32[]{:S(2)}, u32[]{:S(2)}) async-start(bf16[8,512,128]{2,1,0:T(8,128)(2,1)} %bitcast.45), calls=%async_computation | async-start | bytes 2097152 | tf_op jit(solution)/shard_map/all_to_all | solution.py:32
  38.0 34.7 %copy-start.1 = (s32[1,2,160]{2,1,0:T(2,128)S(1)}, s32[1,2,160]{2,1,0:T(2,128)}, u32[]{:S(2)}) copy-start(s32[1,2,160]{2,1,0:T(2,128)} %param.14) | copy-start | bytes 3844
  38.1 34.7 %copy-start.2 = (s32[1,2]{1,0:T(1,128)S(1)}, s32[1,2]{1,0:T(1,128)}, u32[]{:S(2)}) copy-start(s32[1,2]{1,0:T(1,128)} %param.15) | copy-start | bytes 28
  68.5 37.6 %all-to-all-start.1 = ((bf16[8,512,128]{2,1,0:T(8,128)(2,1)}), bf16[8,512,128]{2,1,0:T(8,128)(2,1)S(1)}, u32[]{:S(2)}, u32[]{:S(2)}) async-start(bf16[8,512,128]{2,1,0:T(8,128)(2,1)} %get-tuple-element.12), calls=%async_computation.1 | async-start | bytes 2097152 | tf_op jit(solution)/shard_map/all_to_all | solution.py:36
  72.7 184.0 %all-gather.2.cloned.1.call-start = ((), (), s32[]{:S(2)}) async-start(), calls=%async_computation.3 | async-start | bytes 10485760 | tf_op jit(solution)/shard_map/all_gather | solution.py:44
  195.9 65.0 %copy-start.3 = (f32[256]{0:T(256)S(1)}, f32[256]{0:T(256)}, u32[]{:S(2)}) copy-start(f32[256]{0:T(256)} %param.12) | copy-start | bytes 3076
Sparse Core Ops, SparseCore 0:
  196.1 60.6 all-gather.1
